TPU v7x, 256 devices: a whole 4x4x8 slice. The times are simulated.
256 devices in a mesh: wide: 32 (over x_lo, z, core), rows: 8 (over y, x_hi).
Axes of the slice: x: 4 (x_hi: 2, x_lo: 2; x = x_hi * 2 + x_lo), y: 4, z: 8, core: 2. Of those that a mesh axis runs over, the one named last changes fastest.
Arguments:
- matrix: float32 [8192, 16384], P('rows', 'wide'), may hold values from -600 to 600, as said below
- pairing: int32 [2, 512], replicated, may hold values from 0 to 511, each once within a row
Outputs:
- rotated: float32 [8192, 16384], P('rows', 'wide')
Inputs may be any that keep to these rules, and one draw needn't show every extreme that they name: `matrix`: finite entries.
All inputs are finite; a program needn't handle non-finite values.
Results may differ from a plain program's by a relative error of at most 0.0001.
Values sent between devices are 32-bit elements; how exact they have to be, the bound alone decides.
A program may use at most 64 MiB of HBM per device.

v0:
```python
import jax
import jax.numpy as jnp
from jax import lax
from jax.sharding import PartitionSpec as P

NS_STEPS = 3
EPSILON = 1e-06
HIGH = lax.Precision.HIGHEST


def from_behind(value, axis, steps):
    count = lax.axis_size(axis)
    pairs = [(source, (source + steps) % count) for source in range(count)]
    return lax.ppermute(value, axis, pairs)


def generator(coupling, largest):
    half_cols = coupling.shape[0]
    identity = jnp.eye(half_cols, dtype=jnp.float32)
    top = jnp.concatenate([identity, coupling], axis=1)
    bottom = jnp.concatenate([-coupling.T, identity], axis=1)
    return jnp.concatenate([top, bottom], axis=0) * lax.rsqrt(1.0 + largest)


def shards(matrix, pairing):
    half_cols = matrix.shape[1] // 2
    current = matrix
    for round_index in range(pairing.shape[0]):
        columns = jnp.take(current, pairing[round_index], axis=1)
        partial_value = jnp.einsum(
            "ra,rb->ab", columns, columns, precision=HIGH, preferred_element_type=jnp.float32
        )
        gram = lax.psum(partial_value, "rows")
        norms = jnp.diagonal(gram)
        cross = gram[:half_cols, half_cols:]
        inverse = lax.rsqrt(norms + EPSILON)
        coupling = cross * inverse[:half_cols, None] * inverse[None, half_cols:]
        largest = lax.pmax(jnp.sum(coupling * coupling), "wide")
        rotation = generator(coupling, largest)
        for sweep in range(NS_STEPS):
            square = jnp.einsum(
                "ca,cb->ab", rotation, rotation, precision=HIGH, preferred_element_type=jnp.float32
            )
            rotation = 1.5 * rotation - 0.5 * jnp.dot(
                rotation, square, precision=HIGH, preferred_element_type=jnp.float32
            )
        product = jnp.dot(columns, rotation, precision=HIGH, preferred_element_type=jnp.float32)
        kept_block = product[:, :half_cols]
        moved_block = from_behind(product[:, half_cols:], "wide", 1)
        current = jnp.concatenate([kept_block, moved_block], axis=1)
    return current


def solution(mesh):
    in_specs = (P("rows", "wide"), P())
    out_specs = P("rows", "wide")
    return jax.shard_map(shards, mesh=mesh, in_specs=in_specs, out_specs=out_specs, check_vma=False)
```

profile of v0, /device:TPU:2, one launch (start us, length us, event | category | flops | bytes accessed | tf_op | source)
XLA Modules:
  0.0 418.8 jit_solution(11703738386899458625)
XLA Ops:
  6.5 0.0 all-reduce.3.cloned.1.call-start
  6.5 0.8 fusion.55
  7.3 1.9 copy.12
  9.3 2.7 gather_fusion.2
  11.9 7.0 %fusion.6 = f32[512,512]{1,0:T(8,128)} fusion(f32[512,1024]{1,0:T(8,128)} %gather_fusion.2, pred[512]{0:T(512)(128)(4,1)S(1)} %compare_and_fusion.1), kind=kOutput, calls=%fused_computation.12 | convolution fusion | flops 3221749760 | bytes 3146240 | tf_op jit(solution)/shard_map/ra,rb->ab/dot_general | solution.py:30
  18.9 0.0 all-reduce.3.cloned.1.call-update
  18.9 0.0 all-reduce.5.cloned.1.call-start
  19.0 97.5 %all-reduce.3.cloned.1.call-done = f32[512,512]{1,0:T(8,128)} async-done(((f32[512,512]{1,0:T(8,128)}), f32[512,512]{1,0:T(8,128)}) %all-reduce.3.cloned.1.call-update) | async-done | bytes 1048592 | tf_op jit(solution)/shard_map/psum | solution.py:33
  116.5 8.4 %gather_fusion = f32[512]{0:T(512)S(1)} fusion(f32[512,512]{1,0:T(8,128)} %all-reduce.3.cloned.1.call-done, s32[512]{0:T(512)S(1)} %bitcast.37), kind=kCustom, calls=%fused_computation.2 | custom fusion | bytes 8192 | tf_op jit(solution)/shard_map/jit(diagonal)/cond/branch_0_fun/gather | solution.py:34
  125.0 1.8 multiply_reduce_fusion.1
  126.8 0.1 copy.13
  126.9 54.2 %pmax.14 = f32[]{:T(128)} all-reduce(f32[]{:T(128)} %get-tuple-element.8), channel_id=1, replica_groups=mesh['wide'=32,'rows'=8] {'wide'}, use_global_device_ids=true, to_apply=%region_2.4 | all-reduce | flops 1 | bytes 8 | tf_op jit(solution)/shard_map/pmax | solution.py:38
  181.9 1.9 fusion.33
  183.8 2.0 fusion.17
  185.8 1.9 fusion.58
  187.6 2.0 fusion.16
  189.6 1.9 fusion.59
  191.5 0.0 copy-start
  191.5 1.9 fusion.15
  193.4 0.0 copy-done
  193.4 4.0 fusion.4
  197.4 0.2 fusion.54
  197.6 0.4 collective-permute-start
  198.1 16.0 %collective-permute-done = f32[1024,256]{0,1:T(8,128)S(1)} collective-permute-done((f32[1024,256]{0,1:T(8,128)S(1)}, f32[1024,256]{0,1:T(8,128)S(1)}, u32[]{:S(2)}, u32[]{:S(2)}) %collective-permute-start) | collective-permute-done | bytes 1048608 | tf_op jit(solution)/shard_map/ppermute | solution.py:14
  214.0 0.2 pad_maximum_fusion
  214.3 2.7 gather_fusion.3
  216.9 7.0 %fusion.2 = f32[512,512]{0,1:T(8,128)} fusion(f32[512,1024]{1,0:T(8,128)} %gather_fusion.3, pred[512]{0:T(512)(128)(4,1)S(1)} %compare_and_fusion), kind=kOutput, calls=%fused_computation.8 | convolution fusion | flops 3221749760 | bytes 3146240 | tf_op jit(solution)/shard_map/ra,rb->ab/dot_general | solution.py:30
  224.0 0.0 all-reduce.5.cloned.1.call-update
  224.0 88.2 %all-reduce.5.cloned.1.call-done = f32[512,512]{0,1:T(8,128)} async-done(((f32[512,512]{0,1:T(8,128)}), f32[512,512]{0,1:T(8,128)}) %all-reduce.5.cloned.1.call-update) | async-done | bytes 1048592 | tf_op jit(solution)/shard_map/psum | solution.py:33
  312.2 8.4 %gather_fusion.1 = f32[512]{0:T(512)S(1)} fusion(f32[512,512]{0,1:T(8,128)} %all-reduce.5.cloned.1.call-done, s32[512]{0:T(512)S(1)} %bitcast.38), kind=kCustom, calls=%fused_computation.3 | custom fusion | bytes 8192 | tf_op jit(solution)/shard_map/jit(diagonal)/cond/branch_0_fun/gather | solution.py:34
  320.7 1.8 multiply_reduce_fusion
  322.5 0.1 copy.17
  322.6 54.2 %pmax.15 = f32[]{:T(128)} all-reduce(f32[]{:T(128)} %get-tuple-element.6), channel_id=1, replica_groups=mesh['wide'=32,'rows'=8] {'wide'}, use_global_device_ids=true, to_apply=%region_5.7 | all-reduce | flops 1 | bytes 8 | tf_op jit(solution)/shard_map/pmax | solution.py:38
  377.5 1.9 fusion.30
  379.4 2.0 fusion.14
  381.4 1.9 fusion.60
  383.3 2.0 fusion.13
  385.3 1.9 fusion.61
  387.1 0.0 copy-start.1
  387.1 1.9 fusion.12
  389.0 0.0 copy-done.1
  389.1 4.1 fusion
  393.2 0.2 fusion.53
  393.3 0.4 collective-permute-start.1
  393.8 16.0 %collective-permute-done.1 = f32[1024,256]{0,1:T(8,128)S(1)} collective-permute-done((f32[1024,256]{0,1:T(8,128)S(1)}, f32[1024,256]{0,1:T(8,128)S(1)}, u32[]{:S(2)}, u32[]{:S(2)}) %collective-permute-start.1) | collective-permute-done | bytes 1048608 | tf_op jit(solution)/shard_map/ppermute | solution.py:14
  409.8 0.1 pad_maximum_fusion.1
  409.9 1.8 copy.20
  (14 shorter events, 0.1 us)
Async XLA Ops:
  6.5 110.0 %all-reduce.3.cloned.1.call-start = ((), (), s32[]{:S(2)}) async-start(), calls=%async_computation | async-start | bytes 2097152 | tf_op jit(solution)/shard_map/psum | solution.py:33
  18.9 293.3 %all-reduce.5.cloned.1.call-start = ((), (), s32[]{:S(2)}) async-start(), calls=%async_computation.1 | async-start | bytes 2097152 | tf_op jit(solution)/shard_map/psum | solution.py:33
  191.5 1.9 copy-start
  197.6 16.4 %collective-permute-start = (f32[1024,256]{0,1:T(8,128)S(1)}, f32[1024,256]{0,1:T(8,128)S(1)}, u32[]{:S(2)}, u32[]{:S(2)}) collective-permute-start(f32[1024,256]{0,1:T(8,128)S(1)} %get-tuple-element.13), channel_id=1, source_target_pairs={{0,8},{8,16},{16,24},{24,32},{32,40},{40,48},{48,56},{56,64},{64,7... | collective-permute-start | bytes 3145736 | tf_op jit(solution)/shard_map/ppermute | solution.py:14
  387.1 1.9 copy-start.1
  393.3 16.4 %collective-permute-start.1 = (f32[1024,256]{0,1:T(8,128)S(1)}, f32[1024,256]{0,1:T(8,128)S(1)}, u32[]{:S(2)}, u32[]{:S(2)}) collective-permute-start(f32[1024,256]{0,1:T(8,128)S(1)} %get-tuple-element.11), channel_id=1, source_target_pairs={{0,8},{8,16},{16,24},{24,32},{32,40},{40,48},{48,56},{56,64},{64,7... | collective-permute-start | bytes 3145736 | tf_op jit(solution)/shard_map/ppermute | solution.py:14
Sparse Core Ops, SparseCore 0:
  19.0 97.4 all-reduce.2
  224.1 88.0 all-reduce.4
where the time goes:
time: 424 us; the launch traced here: 419 us
  waiting for transfers between devices  218 us (51%)
  blocking collectives  108 us (25%)
  matrix products  45.1 us (11%)
  local copies, waits for them, and re-layouts  27.3 us (6%)
  between operations  15.4 us (4%)
    psum x2, waiting for transfers between devices, shards(): gram = lax.psum(partial_value, 'rows')  186 us
    pmax x2, blocking collectives, shards(): largest = lax.pmax(jnp.sum(coupling * coupling), 'wide')  108 us
    ppermute x2, waiting for transfers between devices, from_behind(): return lax.ppermute(value, axis, pairs)  32 us
    gather x2, local copies, waits for them, and re-layouts, shards(): norms = jnp.diagonal(gram)  16.8 us
    dot_general x2, matrix products, shards(): jnp.einsum('ra,rb->ab', columns, columns, precision=HIGH, preferred_eleme...  14 us
    dot_general x6, matrix products, shards(): jnp.dot(rotation, square, precision=HIGH, preferred_element_type=jnp.floa...  11.7 us
    dot_general x6, matrix products, shards(): jnp.einsum('ca,cb->ab', rotation, rotation, precision=HIGH, preferred_ele...  11.2 us
  transfers between devices with their start and end apart: 4, of which 4 were waited for; matrix products, arithmetic and copies ran while one was open for 0% of the time, Pallas kernels for 0%

commit v1 on v0

--- a/solution.py
+++ b/solution.py
@@ -1,3 +1,4 @@
+import functools
 import jax
 import jax.numpy as jnp
 from jax import lax
@@ -6,6 +7,14 @@
 NS_STEPS = 3
 EPSILON = 1e-06
 HIGH = lax.Precision.HIGHEST
+
+
+def fit_threads_here(incoming_x, peer_axis):
+    state_now = lax.all_gather(incoming_x, peer_axis)
+    return jnp.sum(state_now, 0)
+
+
+_replace_quarters = functools.partial(fit_threads_here, peer_axis="rows")
 
 
 def from_behind(value, axis, steps):
@@ -30,7 +39,7 @@
         partial_value = jnp.einsum(
             "ra,rb->ab", columns, columns, precision=HIGH, preferred_element_type=jnp.float32
         )
-        gram = lax.psum(partial_value, "rows")
+        gram = _replace_quarters(partial_value)
         norms = jnp.diagonal(gram)
         cross = gram[:half_cols, half_cols:]
         inverse = lax.rsqrt(norms + EPSILON)

time: 424 us -> 462 us (1.090)
  waiting for transfers between devices: 218 us -> 252 us
  local copies, waits for them, and re-layouts: 27.3 us -> 19.6 us
  other arithmetic: 4.03 us -> 11.2 us
  blocking collectives: 108 us -> 113 us
    all_gather x0 -> x2, waiting for transfers between devices: none -> 219 us  [fit_threads_here(): state_now = lax.all_gather(incoming_x, peer_axis)]
    psum x2 -> x0, waiting for transfers between devices: 186 us -> none  [shards(): gram = lax.psum(partial_value, 'rows')]
    reduce_sum x0 -> x2, other arithmetic: none -> 9.06 us  [fit_threads_here(): return jnp.sum(state_now, 0)]
    gather x2, local copies, waits for them, and re-layouts: 16.8 us -> 9.05 us  [shards(): norms = jnp.diagonal(gram)]
    pmax x2, blocking collectives: 108 us -> 113 us  [shards(): largest = lax.pmax(jnp.sum(coupling * coupling), 'wide')]
where the time goes in v1:
time: 462 us; the launch traced here: 456 us
  waiting for transfers between devices  252 us (55%)
  blocking collectives  113 us (24%)
  matrix products  44.9 us (10%)
  local copies, waits for them, and re-layouts  19.6 us (4%)
  between operations  15.2 us (3%)
  other arithmetic  11.2 us (2%)
    all_gather x2, waiting for transfers between devices, fit_threads_here(): state_now = lax.all_gather(incoming_x, peer_axis)  219 us
    pmax x2, blocking collectives, shards(): largest = lax.pmax(jnp.sum(coupling * coupling), 'wide')  113 us
    ppermute x2, waiting for transfers between devices, from_behind(): return lax.ppermute(value, axis, pairs)  32.6 us
    dot_general x2, matrix products, shards(): jnp.einsum('ra,rb->ab', columns, columns, precision=HIGH, preferred_eleme...  14 us
    dot_general x6, matrix products, shards(): jnp.dot(rotation, square, precision=HIGH, preferred_element_type=jnp.floa...  11.5 us
    dot_general x6, matrix products, shards(): jnp.einsum('ca,cb->ab', rotation, rotation, precision=HIGH, preferred_ele...  11.3 us
  transfers between devices with their start and end apart: 4, of which 4 were waited for; matrix products, arithmetic and copies ran while one was open for 0% of the time, Pallas kernels for 0%

profile of v1, /device:TPU:2, one launch (start us, length us, event | category | flops | bytes accessed | tf_op | source)
XLA Modules:
  0.0 456.5 jit_solution(7879933212775961676)
XLA Ops:
  6.5 0.0 all-gather.5.cloned.1.call-start
  6.5 0.8 fusion.55
  7.3 1.9 copy.7
  9.3 2.7 gather_fusion.2
  11.9 7.0 %fusion.6 = f32[512,512]{1,0:T(8,128)} fusion(f32[512,1024]{1,0:T(8,128)} %gather_fusion.2, pred[512]{0:T(512)(128)(4,1)S(1)} %compare_and_fusion.1), kind=kOutput, calls=%fused_computation.12 | convolution fusion | flops 3221749760 | bytes 3146240 | tf_op jit(solution)/shard_map/ra,rb->ab/dot_general | solution.py:39
  18.9 0.0 all-gather.5.cloned.1.call-update
  19.0 0.0 all-gather.7.cloned.1.call-start
  19.1 114.2 %all-gather.5.cloned.1.call-done = f32[4096,512]{1,0:T(8,128)} async-done(((f32[512,512]{1,0:T(8,128)}), f32[4096,512]{1,0:T(8,128)}) %all-gather.5.cloned.1.call-update) | async-done | bytes 8388624 | tf_op jit(solution)/shard_map/all_gather | solution.py:13
  133.3 4.5 reduce_sum.36
  137.8 4.5 gather_fusion
  142.4 0.8 multiply_reduce_fusion.1
  143.2 0.1 copy.8
  143.4 56.7 %pmax.14 = f32[]{:T(128)} all-reduce(f32[]{:T(128)} %get-tuple-element.8), channel_id=1, replica_groups=mesh['wide'=32,'rows'=8] {'wide'}, use_global_device_ids=true, to_apply=%region_2.4 | all-reduce | flops 1 | bytes 8 | tf_op jit(solution)/shard_map/pmax | solution.py:47
  200.7 1.9 fusion.33
  202.6 2.0 fusion.17
  204.5 1.9 fusion.58
  206.5 1.9 fusion.16
  208.4 1.9 fusion.59
  210.2 0.0 copy-start
  210.3 1.9 fusion.15
  212.2 0.0 copy-done
  212.2 4.0 fusion.4
  216.2 0.2 fusion.54
  216.4 0.1 collective-permute-start
  216.6 16.3 %collective-permute-done = f32[1024,256]{0,1:T(8,128)S(1)} collective-permute-done((f32[1024,256]{0,1:T(8,128)S(1)}, f32[1024,256]{0,1:T(8,128)S(1)}, u32[]{:S(2)}, u32[]{:S(2)}) %collective-permute-start) | collective-permute-done | bytes 1048608 | tf_op jit(solution)/shard_map/ppermute | solution.py:23
  232.8 0.2 pad_maximum_fusion
  233.0 2.7 gather_fusion.3
  235.7 7.0 %fusion.2 = f32[512,512]{1,0:T(8,128)} fusion(f32[512,1024]{1,0:T(8,128)} %gather_fusion.3, pred[512]{0:T(512)(128)(4,1)S(1)} %compare_and_fusion), kind=kOutput, calls=%fused_computation.8 | convolution fusion | flops 3221749760 | bytes 3146240 | tf_op jit(solution)/shard_map/ra,rb->ab/dot_general | solution.py:39
  242.7 0.0 all-gather.7.cloned.1.call-update
  242.7 105.0 %all-gather.7.cloned.1.call-done = f32[4096,512]{1,0:T(8,128)} async-done(((f32[512,512]{1,0:T(8,128)}), f32[4096,512]{1,0:T(8,128)}) %all-gather.7.cloned.1.call-update) | async-done | bytes 8388624 | tf_op jit(solution)/shard_map/all_gather | solution.py:13
  347.8 4.5 reduce_sum.38
  352.3 4.5 gather_fusion.1
  356.9 0.8 multiply_reduce_fusion
  357.7 0.1 copy.9
  357.8 56.7 %pmax.15 = f32[]{:T(128)} all-reduce(f32[]{:T(128)} %get-tuple-element.6), channel_id=1, replica_groups=mesh['wide'=32,'rows'=8] {'wide'}, use_global_device_ids=true, to_apply=%region_5.7 | all-reduce | flops 1 | bytes 8 | tf_op jit(solution)/shard_map/pmax | solution.py:47
  415.2 1.9 fusion.30
  417.0 2.0 fusion.14
  419.0 1.9 fusion.60
  420.9 1.9 fusion.13
  422.8 1.9 fusion.61
  424.7 0.0 copy-start.1
  424.7 1.9 fusion.12
  426.6 4.1 fusion
  430.7 0.2 fusion.53
  431.0 0.1 collective-permute-start.1
  431.1 16.3 %collective-permute-done.1 = f32[1024,256]{0,1:T(8,128)S(1)} collective-permute-done((f32[1024,256]{0,1:T(8,128)S(1)}, f32[1024,256]{0,1:T(8,128)S(1)}, u32[]{:S(2)}, u32[]{:S(2)}) %collective-permute-start.1) | collective-permute-done | bytes 1048608 | tf_op jit(solution)/shard_map/ppermute | solution.py:23
  447.4 0.2 pad_maximum_fusion.1
  447.6 1.8 copy.10
  (15 shorter events, 0.1 us)
Async XLA Ops:
  6.5 126.8 %all-gather.5.cloned.1.call-start = ((), (), s32[]{:S(2)}) async-start(), calls=%async_computation | async-start | bytes 9437184 | tf_op jit(solution)/shard_map/all_gather | solution.py:13
  19.0 328.8 %all-gather.7.cloned.1.call-start = ((), (), s32[]{:S(2)}) async-start(), calls=%async_computation.1 | async-start | bytes 9437184 | tf_op jit(solution)/shard_map/all_gather | solution.py:13
  210.2 1.9 copy-start
  216.4 16.4 %collective-permute-start = (f32[1024,256]{0,1:T(8,128)S(1)}, f32[1024,256]{0,1:T(8,128)S(1)}, u32[]{:S(2)}, u32[]{:S(2)}) collective-permute-start(f32[1024,256]{0,1:T(8,128)S(1)} %get-tuple-element.13), channel_id=1, source_target_pairs={{0,8},{8,16},{16,24},{24,32},{32,40},{40,48},{48,56},{56,64},{64,7... | collective-permute-start | bytes 3145736 | tf_op jit(solution)/shard_map/ppermute | solution.py:23
  424.7 1.9 copy-start.1
  431.0 16.4 %collective-permute-start.1 = (f32[1024,256]{0,1:T(8,128)S(1)}, f32[1024,256]{0,1:T(8,128)S(1)}, u32[]{:S(2)}, u32[]{:S(2)}) collective-permute-start(f32[1024,256]{0,1:T(8,128)S(1)} %get-tuple-element.11), channel_id=1, source_target_pairs={{0,8},{8,16},{16,24},{24,32},{32,40},{40,48},{48,56},{56,64},{64,7... | collective-permute-start | bytes 3145736 | tf_op jit(solution)/shard_map/ppermute | solution.py:23
Sparse Core Ops, SparseCore 0:
  19.1 114.1 all-gather.4
  242.8 104.8 all-gather.6
